TPU v7x, 32 devices: a whole 2x2x4 slice. The times are simulated.
32 devices in a mesh: slab: 8 (over z, core), grp: 4 (over y, x).
Axes of the slice: x: 2, y: 2, z: 4, core: 2. Of those that a mesh axis runs over, the one named last changes fastest.
Arguments:
- stress: bfloat16 [6, 262144], P(None, ('slab', 'grp')), may hold values from -6 to 6
- interp_weight: bfloat16 [2048, 64, 128], P(('slab', 'grp')), may hold values from -0.5 to 0.5
- block_owner: int32 [2048, 1], P(('slab', 'grp')), may hold values from 0 to 3; in each aligned block of 64 rows (0 to 63, 64 to 127, ...) at most 48 rows name the same one
- block_local: int32 [2048], P(('slab', 'grp')), may hold values from 0 to 63
- slip_system: int32 [131072], P(('slab', 'grp')), may hold values from 0 to 11
- mobility: float32 [131072], P(('slab', 'grp')), may hold values from 0.3 to 3
- position: float32 [3, 131072], P(None, ('slab', 'grp')), may hold values from -6 to 6
- target_slab: int32 [131072, 1], P(('slab', 'grp')), may hold values from 0 to 7; in each aligned block of 4096 rows (0 to 4095, 4096 to 8191, ...) at most 1024 rows name the same one
Outputs:
- distortion: float32 [6, 262144], P(None, ('slab', 'grp'))
- arrived: float32 [4, 262144], P(None, ('slab', 'grp'))
Inputs may be any that keep to these rules, and one draw needn't show every extreme that they name: Among the 64 segment blocks of one device at most 48 have the same block_owner; on some device exactly 48 do. Among the 4096 segments of one device at most 1024 have the same target_slab; on some device exactly 1024 do.
All inputs are finite; a program needn't handle non-finite values.
Results may differ from a plain program's by a relative error of at most 0.01.
Values may be sent and summed in bfloat16 or wider, within the bound.
No kernel may reach another device: no remote copies, remote signals or barrier semaphores. Data moves between devices by JAX's collectives and lax.ppermute only.
A program may use at most 64 MiB of HBM per device.

v0:
```python
import jax
import jax.numpy as jnp
import numpy as np
from jax import lax
from jax.sharding import PartitionSpec as P

NC = 6
NSYS = 12
BLK = 128
SEGB = 64
glide_time = 0.5


def slip_tables():
    normal_list = [(1.0, 1.0, 1.0), (-1.0, 1.0, 1.0), (1.0, -1.0, 1.0), (1.0, 1.0, -1.0)]
    schmid_rows = []
    glide_rows = []
    for along_x, along_y, along_z in normal_list:
        normal_vec = np.array([along_x, along_y, along_z]) / np.sqrt(3.0)
        for burgers in (
            (along_y, -along_x, 0.0),
            (along_z, 0.0, -along_x),
            (0.0, along_z, -along_y),
        ):
            burgers_vec = np.array(burgers) / np.sqrt(2.0)
            tensor = 0.5 * (np.outer(normal_vec, burgers_vec) + np.outer(burgers_vec, normal_vec))
            schmid_rows.append(
                [
                    tensor[0, 0],
                    tensor[1, 1],
                    tensor[2, 2],
                    2.0 * tensor[1, 2],
                    2.0 * tensor[0, 2],
                    2.0 * tensor[0, 1],
                ]
            )
            glide_rows.append(burgers_vec)
    return (np.array(schmid_rows, np.float32).T, np.array(glide_rows, np.float32).T)


def slot_ranks(labels, count):
    onehot = (labels[:, None] == jnp.arange(count, dtype=jnp.int32)[None, :]).astype(jnp.int32)
    return jnp.sum((jnp.cumsum(onehot, axis=0) - onehot) * onehot, axis=1)


def body(
    stress, interp_weight, block_owner, block_local, slip_system, mobility, position, target_slab
):
    schmid_np, glide_np = slip_tables()
    schmid = jnp.asarray(schmid_np, jnp.float32)
    glide_table = jnp.asarray(glide_np, jnp.float32)
    group_size = lax.axis_size("grp")
    slab_count = lax.axis_size("slab")
    block_count = interp_weight.shape[0]
    local_blocks = stress.shape[1] // BLK
    owner_index = block_owner[:, 0]
    slab_stress = lax.all_gather(stress, "grp", axis=1, tiled=True)
    stress_tiles = slab_stress.reshape(NC, group_size * local_blocks, BLK)[
        :, owner_index * local_blocks + block_local, :
    ]
    sampled = jnp.einsum(
        "cbv,bsv->cbs", stress_tiles, interp_weight, preferred_element_type=jnp.float32
    ).reshape(NC, -1)
    systems_hot = (jnp.arange(NSYS, dtype=jnp.int32)[:, None] == slip_system[None, :]).astype(
        jnp.float32
    )
    factors = jnp.dot(schmid, systems_hot, precision=lax.Precision.HIGHEST)
    resolved = jnp.sum(factors * sampled, axis=0)
    glide_step = glide_time * mobility * resolved
    weight_term = (
        (glide_step[None, :] * factors).astype(jnp.bfloat16).reshape(NC, block_count, SEGB)
    )
    spread = jnp.einsum(
        "cbs,bsv->cbv", weight_term, interp_weight, preferred_element_type=jnp.float32
    )
    dense_term = (
        jnp.zeros((NC, group_size * local_blocks, BLK), jnp.float32)
        .at[:, owner_index * local_blocks + block_local, :]
        .add(spread)
    )
    distortion = lax.psum_scatter(
        dense_term.reshape(NC, -1).astype(jnp.bfloat16), "grp", scatter_dimension=1, tiled=True
    ).astype(jnp.float32)
    glide_dirs = jnp.dot(glide_table, systems_hot, precision=lax.Precision.HIGHEST)
    moved_position = position + glide_dirs * glide_step[None, :]
    payload = jnp.concatenate([moved_position, glide_step[None, :]], axis=0)
    target = target_slab[:, 0]
    target_rank = slot_ranks(target, slab_count)
    per_peer = 2 * payload.shape[1] // slab_count
    outgoing_moves = (
        jnp.zeros((4, slab_count, per_peer), jnp.float32).at[:, target, target_rank].set(payload)
    )
    arrived = (
        lax.all_to_all(
            outgoing_moves.astype(jnp.bfloat16), "slab", split_axis=1, concat_axis=1, tiled=True
        )
        .astype(outgoing_moves.dtype)
        .reshape(4, -1)
    )
    return (distortion, arrived)


def solution(mesh):
    placed = (
        P(None, ("slab", "grp")),
        P(("slab", "grp"), None, None),
        P(("slab", "grp"), None),
        P(("slab", "grp")),
        P(("slab", "grp")),
        P(("slab", "grp")),
        P(None, ("slab", "grp")),
        P(("slab", "grp"), None),
    )
    return jax.shard_map(
        body,
        mesh=mesh,
        in_specs=placed,
        out_specs=(P(None, ("slab", "grp")), P(None, ("slab", "grp"))),
        check_vma=False,
    )
```

profile of v0, /device:TPU:0, one launch (start us, length us, event | category | flops | bytes accessed | tf_op | source)
XLA Modules:
  0.0 67.4 jit_solution(1898360276803271494)
XLA Ops:
  7.2 0.8 %compare_select_fusion.2 = s32[64]{0:T(128)S(1)} fusion(s32[64]{0:T(128)} %param.13, s32[64,1]{0,1:T(1,128)} %param.12), kind=kLoop, calls=%fused_computation.37 | loop fusion | flops 320 | bytes 768 | tf_op jit(solution)/shard_map/select_n | solution.py:79
  8.0 11.8 %all_gather.3 = bf16[6,32768]{1,0:T(8,128)(2,1)S(1)} all-gather(bf16[6,8192]{1,0:T(8,128)(2,1)} %param.10), channel_id=1, replica_groups=mesh['slab'=8,'grp'=4] {'grp'}, dimensions={1}, use_global_device_ids=true | all-gather | bytes 491520 | tf_op jit(solution)/shard_map/all_gather | solution.py:57
  19.8 0.6 gather_fusion
  20.5 0.6 convolution_bitcast_fusion
  21.3 1.0 %multiply_reduce_fusion = (f32[4096]{0:T(1024)S(1)}, f32[6,4096]{1,0:T(8,128)S(1)}) fusion(f32[6,4096]{1,0:T(8,128)S(1)} %reshape.55, f32[6,12]{1,0:T(8,128)} %constant.7.clone, s32[4096]{0:T(1024)} %param.14), kind=kOutput, calls=%fused_computation.24 | convolution fusion | flops 3633152 | bytes 229664 | tf_op jit(solution)/shard_map/dot_general | solution.py:67
  22.3 0.7 %multiply_multiply_fusion = f32[4096]{0:T(1024)S(1)} fusion(f32[4096]{0:T(1024)S(1)} %get-tuple-element.2, f32[4096]{0:T(1024)} %param.15), kind=kLoop, calls=%fused_computation.34 | loop fusion | flops 8192 | bytes 49152 | tf_op jit(solution)/shard_map/mul | solution.py:69
  23.2 0.4 fusion.9
  23.6 2.7 %scatter_fusion = f32[6,256,128]{2,0,1:T(8,128)S(1)} fusion(f32[6,256,128]{2,0,1:T(8,128)S(1)} %broadcast_in_dim.8, s32[64]{0:T(128)S(1)} %compare_select_fusion.2, f32[64,6,128]{2,1,0:T(8,128)S(1)} %fusion.9), kind=kCustom, calls=%fused_computation.1 | custom fusion | flops 49152 | bytes 590080 | tf_op jit(solution)/shard_map/scatter-add | solution.py:79
  26.4 0.9 %convert_bitcast_fusion = bf16[6,32768]{1,0:T(8,128)(2,1)} fusion(f32[6,256,128]{2,0,1:T(8,128)S(1)} %scatter_fusion), kind=kLoop, calls=%fused_computation.9 | loop fusion | flops 196608 | bytes 1179648 | tf_op jit(solution)/shard_map/convert_element_type | solution.py:82
  27.3 2.3 %reduce-window.6 = s32[8,32,128]{2,1,0:T(8,128)S(1)} reduce-window(s32[8,32,128]{2,1,0:T(8,128)S(1)} %fusion.13, s32[]{:T(128)} %constant.11.clone.1), window={size=1x1x128 pad=0_0x0_0x127_0}, to_apply=%region_3.0 | reduce-window | flops 4161536 | bytes 262148 | tf_op jit(solution)/shard_map/reduce-window
  29.6 0.3 slice_reduce_fusion
  29.9 0.2 reduce-window.9
  30.1 0.1 add_bitcast_fusion
  30.2 0.1 fusion.7
  30.4 0.2 fusion.1
  30.7 0.6 copy.22
  31.3 0.1 multiply_reduce_fusion.1
  31.4 0.1 and_reduce_fusion
  31.6 12.8 %scatter_custom_fusion.1 = f32[4,8192]{0,1:T(8,128)} fusion(s32[4096]{0:T(1024)S(1)} %broadcast_select_fusion, f32[4096,4]{1,0:T(8,128)S(1)} %copy.22, f32[]{:T(128)} %constant.9.clone.1), kind=kCustom, calls=%fused_computation.6 | custom fusion | bytes 131076
  44.3 2.4 %convert_element_type.31 = bf16[4,8192]{0,1:T(8,128)(2,1)S(1)} convert(f32[4,8192]{0,1:T(8,128)} %scatter_custom_fusion.1) | non-fusion elementwise | flops 32768 | bytes 196608 | tf_op jit(solution)/shard_map/convert_element_type | solution.py:95
  46.7 0.9 %copy.23 = bf16[4,8,1024]{2,0,1:T(4,128)(2,1)S(1)} copy(bf16[4,8,1024]{0,2,1:T(8,128)(2,1)S(1)} %bitcast.48) | data formatting | bytes 131072 | tf_op jit(solution)/shard_map/convert_element_type | solution.py:95
  47.6 10.6 %all_to_all.5 = bf16[4,8,1024]{2,0,1:T(4,128)(2,1)S(1)} all-to-all(bf16[4,8,1024]{2,0,1:T(4,128)(2,1)S(1)} %copy.23), channel_id=1, replica_groups=mesh['slab'=8,'grp'=4] {'slab'}, dimensions={1} | all-to-all | bytes 131072 | tf_op jit(solution)/shard_map/all_to_all | solution.py:94
  58.2 0.7 convert.1
  58.9 1.6 %convert_element_type.27 = f32[6,8192]{1,0:T(8,128)} convert(bf16[6,8192]{1,0:T(8,128)(2,1)} %reduce-scatter.2.cloned.1.call-done) | non-fusion elementwise | flops 49152 | bytes 294912 | tf_op jit(solution)/shard_map/convert_element_type | solution.py:83
  (27 shorter events, 0.5 us)
Async XLA Ops:
  7.2 13.3 %copy-start = (bf16[64,64,128]{2,1,0:T(8,128)(2,1)S(1)}, bf16[64,64,128]{2,1,0:T(8,128)(2,1)}, u32[]{:S(2)}) copy-start(bf16[64,64,128]{2,1,0:T(8,128)(2,1)} %param.11) | copy-start | bytes 3145732
  7.2 51.7 %reduce-scatter.2.cloned.1.call-start = ((), (), s32[]{:S(2)}) async-start(), calls=%async_computation.2 | async-start | bytes 655360 | tf_op jit(solution)/shard_map/reduce_scatter | solution.py:81
  20.5 6.8 %copy-start.1 = (s32[4096,1]{0,1:T(1,128)S(1)}, s32[4096,1]{0,1:T(1,128)}, u32[]{:S(2)}) copy-start(s32[4096,1]{0,1:T(1,128)} %param.17) | copy-start | bytes 49156
  21.1 9.2 %copy-start.2 = (f32[3,4096]{1,0:T(4,128)S(1)}, f32[3,4096]{1,0:T(4,128)}, u32[]{:S(2)}) copy-start(f32[3,4096]{1,0:T(4,128)} %param.16) | copy-start | bytes 147460
  21.1 9.2 %copy-start.3 = (s32[4096]{0:T(1024)S(1)}, s32[4096]{0:T(1024)}, u32[]{:S(2)}) copy-start(s32[4096]{0:T(1024)} %param.14) | copy-start | bytes 49156
  21.1 9.3 %copy-start.4 = (f32[3,12]{1,0:T(4,128)S(1)}, f32[3,12]{1,0:T(4,128)}, u32[]{:S(2)}) copy-start(f32[3,12]{1,0:T(4,128)} %constant.8.clone) | copy-start | bytes 436
  23.1 8.2 %copy-start.6 = (s32[2]{0:T(128)S(1)}, s32[2]{0:T(128)}, u32[]{:S(2)}) copy-start(s32[2]{0:T(128)} %constant.28) | copy-start | bytes 28
  23.1 8.3 %copy-start.5 = (s32[2]{0:T(128)S(1)}, s32[2]{0:T(128)}, u32[]{:S(2)}) copy-start(s32[2]{0:T(128)} %constant.31) | copy-start | bytes 28
Sparse Core Ops, SparseCore 0:
  27.4 25.0 reduce-scatter.1
where the time goes:
time: 67.8 us; the launch traced here: 67.4 us
  blocking collectives  22.4 us (33%)
  local copies, waits for them, and re-layouts  15.6 us (23%)
  between operations  14.2 us (21%)
  other arithmetic  12.8 us (19%)
  matrix products  2.21 us (3%)
    unnamed x15, local copies, waits for them, and re-layouts  12.8 us
    all_gather x1, blocking collectives, body(): slab_stress = lax.all_gather(stress, 'grp', axis=1, tiled=True)  11.8 us
    all_to_all x1, blocking collectives, body(): lax.all_to_all(outgoing_moves.astype(jnp.bfloat16), 'slab', split_axis=1,...  10.6 us
    scatter-add x1, other arithmetic, body(): dense_term = jnp.zeros((NC, group_size * local_blocks, BLK), jnp.float32)...  2.74 us
    another operation x2, other arithmetic  2.5 us
    convert_element_type x1, other arithmetic, body(): outgoing_moves.astype(jnp.bfloat16)  2.39 us
    convert_element_type x1, other arithmetic, body(): distortion = lax.psum_scatter(dense_term.reshape(NC, -1).astype(jnp.bfloa...  1.62 us
  transfers between devices with their start and end apart: 1, of which 0 were waited for; matrix products, arithmetic and copies ran while one was open for 31% of the time, Pallas kernels for 0%

commit v1 on v0

--- a/solution.py
+++ b/solution.py
@@ -3,12 +3,31 @@
 import numpy as np
 from jax import lax
 from jax.sharding import PartitionSpec as P
+from jax.lax import axis_index, axis_size, ppermute
 
 NC = 6
 NSYS = 12
 BLK = 128
 SEGB = 64
 glide_time = 0.5
+
+
+def part_series_in(mine):
+    built = axis_size("slab")
+    row_out = axis_index("slab")
+    later, main = (built, row_out)
+    clean = mine.shape[1] // later
+    even = list(mine.shape)
+    even[1] = clean
+    formed = even[1]
+    even[1] = formed * later
+    newest = jnp.zeros(even, mine.dtype)
+    for kk in range(later):
+        v_now = lax.dynamic_slice_in_dim(mine, (main ^ kk) * clean, clean, axis=1)
+        if kk:
+            v_now = ppermute(v_now, "slab", [(ix, ix ^ kk) for ix in range(later)])
+        newest = lax.dynamic_update_slice_in_dim(newest, v_now, (main ^ kk) * formed, axis=1)
+    return newest
 
 
 def slip_tables():
@@ -91,9 +110,7 @@
         jnp.zeros((4, slab_count, per_peer), jnp.float32).at[:, target, target_rank].set(payload)
     )
     arrived = (
-        lax.all_to_all(
-            outgoing_moves.astype(jnp.bfloat16), "slab", split_axis=1, concat_axis=1, tiled=True
-        )
+        part_series_in(outgoing_moves.astype(jnp.bfloat16))
         .astype(outgoing_moves.dtype)
         .reshape(4, -1)
     )

time: 67.8 us -> 107 us (1.58)
  the two profiles are of different devices: /device:TPU:0 before, /device:TPU:17 now
where the time goes in v1:
time: 107 us
  waiting for transfers between devices  41 us (38%)
  local copies, waits for them, and re-layouts  19.1 us (18%)
  between operations  14.4 us (13%)
  other arithmetic  12.2 us (11%)
  starting transfers between devices  9.07 us (8%)
  blocking collectives  8.95 us (8%)
  matrix products  2.21 us (2%)
    ppermute x7, waiting for transfers between devices, part_series_in(): v_now = ppermute(v_now, 'slab', [(ix, ix ^ kk) for ix in range(later)])  41 us
    unnamed x16, local copies, waits for them, and re-layouts  13.5 us
    ppermute x7, starting transfers between devices, part_series_in(): v_now = ppermute(v_now, 'slab', [(ix, ix ^ kk) for ix in range(later)])  9.03 us
    all_gather x1, blocking collectives, body(): slab_stress = lax.all_gather(stress, 'grp', axis=1, tiled=True)  8.95 us
    scatter-add x1, other arithmetic, body(): dense_term = jnp.zeros((NC, group_size * local_blocks, BLK), jnp.float32)...  2.73 us
    another operation x2, other arithmetic  2.5 us
    convert_element_type x1, other arithmetic, body(): outgoing_moves.astype(jnp.bfloat16)  2.39 us
  transfers between devices with their start and end apart: 8, of which 5 were waited for; matrix products, arithmetic and copies ran while one was open for 22% of the time, Pallas kernels for 0%

profile of v1, /device:TPU:17, one launch (start us, length us, event | category | flops | bytes accessed | tf_op | source)
XLA Modules:
  0.0 106.9 jit_solution(13618398128275697702)
XLA Ops:
  7.2 0.8 compare_select_fusion.2
  8.0 9.0 %all_gather.3 = bf16[6,32768]{1,0:T(8,128)(2,1)S(1)} all-gather(bf16[6,8192]{1,0:T(8,128)(2,1)} %param.10), channel_id=1, replica_groups=mesh['slab'=8,'grp'=4] {'grp'}, dimensions={1}, use_global_device_ids=true | all-gather | bytes 491520 | tf_op jit(solution)/shard_map/all_gather | solution.py:76
  16.9 0.6 gather_fusion
  17.6 0.6 convolution_bitcast_fusion
  18.4 1.0 multiply_reduce_fusion
  19.4 0.7 multiply_multiply_fusion
  20.7 2.7 %scatter_fusion = f32[6,256,128]{2,0,1:T(8,128)S(1)} fusion(f32[6,256,128]{2,0,1:T(8,128)S(1)} %broadcast_in_dim.10, s32[64]{0:T(128)S(1)} %compare_select_fusion.2, f32[64,6,128]{2,1,0:T(8,128)S(1)} %fusion.9), kind=kCustom, calls=%fused_computation.1 | custom fusion | flops 49152 | bytes 590080 | tf_op jit(solution)/shard_map/scatter-add | solution.py:98
  23.5 0.9 convert_bitcast_fusion
  24.4 2.3 %reduce-window.6 = s32[8,32,128]{2,1,0:T(8,128)S(1)} reduce-window(s32[8,32,128]{2,1,0:T(8,128)S(1)} %fusion.13, s32[]{:T(128)} %constant.21.clone.1), window={size=1x1x128 pad=0_0x0_0x127_0}, to_apply=%region_3.0 | reduce-window | flops 4161536 | bytes 262148 | tf_op jit(solution)/shard_map/reduce-window
  27.9 0.6 copy.25
  28.7 12.8 %scatter_custom_fusion.1 = f32[4,8192]{0,1:T(8,128)} fusion(s32[4096]{0:T(1024)S(1)} %broadcast_select_fusion, f32[4096,4]{1,0:T(8,128)S(1)} %copy.25, f32[]{:T(128)} %constant.19.clone.1), kind=kCustom, calls=%fused_computation.6 | custom fusion | bytes 131076
  41.5 2.4 %convert_element_type.31 = bf16[4,8192]{0,1:T(8,128)(2,1)S(1)} convert(f32[4,8192]{0,1:T(8,128)} %scatter_custom_fusion.1) | non-fusion elementwise | flops 32768 | bytes 196608 | tf_op jit(solution)/shard_map/convert_element_type | solution.py:113
  43.9 1.1 %constant_dynamic-slice_fusion = (bf16[4,1,1024]{0,2,1:T(8,128)(2,1)}, bf16[4,1,1024]{0,2,1:T(8,128)(2,1)}, bf16[4,1,1024]{0,2,1:T(8,128)(2,1)}, bf16[4,1,1024]{...) fusion(bf16[4,8,1024]{0,2,1:T(8,128)(2,1)S(1)} %bitcast.49, ...), kind=kLoop, calls=%fused_computation.39 | loop fusion | bytes 131104 | tf_op jit(solution)/shard_map/dynamic_slice | solution.py:26
  45.0 2.1 %collective-permute-start = (bf16[4,1,1024]{0,2,1:T(8,128)(2,1)S(1)}, bf16[4,1,1024]{0,2,1:T(8,128)(2,1)S(1)}, u32[]{:S(2)}, u32[]{:S(2)}) collective-permute-start(bf16[4,1,1024]{0,2,1:T(8,128)(2,1)S(1)} %get-tuple-element.8), channel_id=1, source_target_pairs={{0,4},{4,0},{8,12},{12,8},{16,20},{20,16},{24,28},{28,24},{1,5},{5... | collective-permute-start | bytes 24584 | tf_op jit(solution)/shard_map/ppermute | solution.py:28
  47.1 1.3 %collective-permute-start.1 = (bf16[4,1,1024]{0,2,1:T(8,128)(2,1)S(1)}, bf16[4,1,1024]{0,2,1:T(8,128)(2,1)S(1)}, u32[]{:S(2)}, u32[]{:S(2)}) collective-permute-start(bf16[4,1,1024]{0,2,1:T(8,128)(2,1)S(1)} %get-tuple-element.7), channel_id=1, source_target_pairs={{0,8},{4,12},{8,0},{12,4},{16,24},{20,28},{24,16},{28,20},{1,9},{5... | collective-permute-start | bytes 24584 | tf_op jit(solution)/shard_map/ppermute | solution.py:28
  48.8 2.7 %collective-permute-start.4 = (bf16[4,1,1024]{0,2,1:T(8,128)(2,1)}, bf16[4,1,1024]{0,2,1:T(8,128)(2,1)S(1)}, u32[]{:S(2)}, u32[]{:S(2)}) collective-permute-start(bf16[4,1,1024]{0,2,1:T(8,128)(2,1)} %get-tuple-element.4), channel_id=1, source_target_pairs={{0,20},{4,16},{8,28},{12,24},{16,4},{20,0},{24,12},{28,8},{1,21},{... | collective-permute-start | bytes 24584 | tf_op jit(solution)/shard_map/ppermute | solution.py:28
  51.7 10.8 %collective-permute-done.1 = bf16[4,1,1024]{0,2,1:T(8,128)(2,1)S(1)} collective-permute-done((bf16[4,1,1024]{0,2,1:T(8,128)(2,1)S(1)}, bf16[4,1,1024]{0,2,1:T(8,128)(2,1)S(1)}, u32[]{:S(2)}, u32[]{:S(2)}) %collective-permute-start.1) | collective-permute-done | bytes 8224 | tf_op jit(solution)/shard_map/ppermute | solution.py:28
  62.5 2.3 %collective-permute-start.6 = (bf16[4,1,1024]{0,2,1:T(8,128)(2,1)}, bf16[4,1,1024]{0,2,1:T(8,128)(2,1)S(1)}, u32[]{:S(2)}, u32[]{:S(2)}) collective-permute-start(bf16[4,1,1024]{0,2,1:T(8,128)(2,1)} %get-tuple-element.2), channel_id=1, source_target_pairs={{0,28},{4,24},{8,20},{12,16},{16,12},{20,8},{24,4},{28,0},{1,29},{... | collective-permute-start | bytes 24584 | tf_op jit(solution)/shard_map/ppermute | solution.py:28
  65.8 2.4 %collective-permute-done.2 = bf16[4,1,1024]{0,2,1:T(8,128)(2,1)S(1)} collective-permute-done((bf16[4,1,1024]{0,2,1:T(8,128)(2,1)}, bf16[4,1,1024]{0,2,1:T(8,128)(2,1)S(1)}, u32[]{:S(2)}, u32[]{:S(2)}) %collective-permute-start.2) | collective-permute-done | bytes 8224 | tf_op jit(solution)/shard_map/ppermute | solution.py:28
  68.8 3.5 %collective-permute-done.4 = bf16[4,1,1024]{0,2,1:T(8,128)(2,1)S(1)} collective-permute-done((bf16[4,1,1024]{0,2,1:T(8,128)(2,1)}, bf16[4,1,1024]{0,2,1:T(8,128)(2,1)S(1)}, u32[]{:S(2)}, u32[]{:S(2)}) %collective-permute-start.4) | collective-permute-done | bytes 8224 | tf_op jit(solution)/shard_map/ppermute | solution.py:28
  72.7 18.7 %collective-permute-done.5 = bf16[4,1,1024]{0,2,1:T(8,128)(2,1)S(1)} collective-permute-done((bf16[4,1,1024]{0,2,1:T(8,128)(2,1)}, bf16[4,1,1024]{0,2,1:T(8,128)(2,1)S(1)}, u32[]{:S(2)}, u32[]{:S(2)}) %collective-permute-start.5) | collective-permute-done | bytes 8224 | tf_op jit(solution)/shard_map/ppermute | solution.py:28
  91.7 5.6 %collective-permute-done.6 = bf16[4,1,1024]{0,2,1:T(8,128)(2,1)S(1)} collective-permute-done((bf16[4,1,1024]{0,2,1:T(8,128)(2,1)}, bf16[4,1,1024]{0,2,1:T(8,128)(2,1)S(1)}, u32[]{:S(2)}, u32[]{:S(2)}) %collective-permute-start.6) | collective-permute-done | bytes 8224 | tf_op jit(solution)/shard_map/ppermute | solution.py:28
  97.7 0.7 copy.35
  98.5 1.6 %convert_element_type.27 = f32[6,8192]{1,0:T(8,128)} convert(bf16[6,8192]{1,0:T(8,128)(2,1)} %reduce-scatter.2.cloned.1.call-done) | non-fusion elementwise | flops 49152 | bytes 294912 | tf_op jit(solution)/shard_map/convert_element_type | solution.py:102
  (58 shorter events, 5.2 us)
Async XLA Ops:
  7.2 10.4 %copy-start = (bf16[64,64,128]{2,1,0:T(8,128)(2,1)S(1)}, bf16[64,64,128]{2,1,0:T(8,128)(2,1)}, u32[]{:S(2)}) copy-start(bf16[64,64,128]{2,1,0:T(8,128)(2,1)} %param.11) | copy-start | bytes 3145732
  7.2 91.3 %reduce-scatter.2.cloned.1.call-start = ((), (), s32[]{:S(2)}) async-start(), calls=%async_computation.1 | async-start | bytes 655360 | tf_op jit(solution)/shard_map/reduce_scatter | solution.py:100
  17.6 6.8 %copy-start.1 = (s32[4096,1]{0,1:T(1,128)S(1)}, s32[4096,1]{0,1:T(1,128)}, u32[]{:S(2)}) copy-start(s32[4096,1]{0,1:T(1,128)} %param.17) | copy-start | bytes 49156
  18.2 9.2 %copy-start.2 = (f32[3,4096]{1,0:T(4,128)S(1)}, f32[3,4096]{1,0:T(4,128)}, u32[]{:S(2)}) copy-start(f32[3,4096]{1,0:T(4,128)} %param.16) | copy-start | bytes 147460
  18.2 9.2 %copy-start.3 = (s32[4096]{0:T(1024)S(1)}, s32[4096]{0:T(1024)}, u32[]{:S(2)}) copy-start(s32[4096]{0:T(1024)} %param.14) | copy-start | bytes 49156
  18.2 9.2 %copy-start.4 = (f32[3,12]{1,0:T(4,128)S(1)}, f32[3,12]{1,0:T(4,128)}, u32[]{:S(2)}) copy-start(f32[3,12]{1,0:T(4,128)} %constant.50.clone) | copy-start | bytes 436
  18.2 9.5 %copy-start.6 = (s32[2]{0:T(128)S(1)}, s32[2]{0:T(128)}, u32[]{:S(2)}) copy-start(s32[2]{0:T(128)} %constant.51) | copy-start | bytes 28
  20.2 8.3 %copy-start.5 = (s32[2]{0:T(128)S(1)}, s32[2]{0:T(128)}, u32[]{:S(2)}) copy-start(s32[2]{0:T(128)} %constant.54) | copy-start | bytes 28
  45.0 6.5 %collective-permute-start = (bf16[4,1,1024]{0,2,1:T(8,128)(2,1)S(1)}, bf16[4,1,1024]{0,2,1:T(8,128)(2,1)S(1)}, u32[]{:S(2)}, u32[]{:S(2)}) collective-permute-start(bf16[4,1,1024]{0,2,1:T(8,128)(2,1)S(1)} %get-tuple-element.8), channel_id=1, source_target_pairs={{0,4},{4,0},{8,12},{12,8},{16,20},{20,16},{24,28},{28,24},{1,5},{5... | collective-permute-start | bytes 24584 | tf_op jit(solution)/shard_map/ppermute | solution.py:28
  47.1 15.4 %collective-permute-start.1 = (bf16[4,1,1024]{0,2,1:T(8,128)(2,1)S(1)}, bf16[4,1,1024]{0,2,1:T(8,128)(2,1)S(1)}, u32[]{:S(2)}, u32[]{:S(2)}) collective-permute-start(bf16[4,1,1024]{0,2,1:T(8,128)(2,1)S(1)} %get-tuple-element.7), channel_id=1, source_target_pairs={{0,8},{4,12},{8,0},{12,4},{16,24},{20,28},{24,16},{28,20},{1,9},{5... | collective-permute-start | bytes 24584 | tf_op jit(solution)/shard_map/ppermute | solution.py:28
  48.4 19.8 %collective-permute-start.2 = (bf16[4,1,1024]{0,2,1:T(8,128)(2,1)}, bf16[4,1,1024]{0,2,1:T(8,128)(2,1)S(1)}, u32[]{:S(2)}, u32[]{:S(2)}) collective-permute-start(bf16[4,1,1024]{0,2,1:T(8,128)(2,1)} %get-tuple-element.6), channel_id=1, source_target_pairs={{0,12},{4,8},{8,4},{12,0},{16,28},{20,24},{24,20},{28,16},{1,13},{... | collective-permute-start | bytes 24584 | tf_op jit(solution)/shard_map/ppermute | solution.py:28
  48.7 19.8 %collective-permute-start.3 = (bf16[4,1,1024]{0,2,1:T(8,128)(2,1)}, bf16[4,1,1024]{0,2,1:T(8,128)(2,1)S(1)}, u32[]{:S(2)}, u32[]{:S(2)}) collective-permute-start(bf16[4,1,1024]{0,2,1:T(8,128)(2,1)} %get-tuple-element.5), channel_id=1, source_target_pairs={{0,16},{4,20},{8,24},{12,28},{16,0},{20,4},{24,8},{28,12},{1,17},{... | collective-permute-start | bytes 24584 | tf_op jit(solution)/shard_map/ppermute | solution.py:28
  48.8 23.6 %collective-permute-start.4 = (bf16[4,1,1024]{0,2,1:T(8,128)(2,1)}, bf16[4,1,1024]{0,2,1:T(8,128)(2,1)S(1)}, u32[]{:S(2)}, u32[]{:S(2)}) collective-permute-start(bf16[4,1,1024]{0,2,1:T(8,128)(2,1)} %get-tuple-element.4), channel_id=1, source_target_pairs={{0,20},{4,16},{8,28},{12,24},{16,4},{20,0},{24,12},{28,8},{1,21},{... | collective-permute-start | bytes 24584 | tf_op jit(solution)/shard_map/ppermute | solution.py:28
  51.5 39.9 %collective-permute-start.5 = (bf16[4,1,1024]{0,2,1:T(8,128)(2,1)}, bf16[4,1,1024]{0,2,1:T(8,128)(2,1)S(1)}, u32[]{:S(2)}, u32[]{:S(2)}) collective-permute-start(bf16[4,1,1024]{0,2,1:T(8,128)(2,1)} %get-tuple-element.3), channel_id=1, source_target_pairs={{0,24},{4,28},{8,16},{12,20},{16,8},{20,12},{24,0},{28,4},{1,25},{... | collective-permute-start | bytes 24584 | tf_op jit(solution)/shard_map/ppermute | solution.py:28
  62.5 34.9 %collective-permute-start.6 = (bf16[4,1,1024]{0,2,1:T(8,128)(2,1)}, bf16[4,1,1024]{0,2,1:T(8,128)(2,1)S(1)}, u32[]{:S(2)}, u32[]{:S(2)}) collective-permute-start(bf16[4,1,1024]{0,2,1:T(8,128)(2,1)} %get-tuple-element.2), channel_id=1, source_target_pairs={{0,28},{4,24},{8,20},{12,16},{16,12},{20,8},{24,4},{28,0},{1,29},{... | collective-permute-start | bytes 24584 | tf_op jit(solution)/shard_map/ppermute | solution.py:28
Sparse Core Ops, SparseCore 0:
  24.5 26.1 reduce-scatter.1
